TPU v7x, 32 devices: a whole 2x2x4 slice. The times are simulated.
32 devices in a mesh: group: 2 (over core), dp: 4 (over z), section: 2 (over x), tensor: 2 (over y).
Axes of the slice: x: 2, y: 2, z: 4, core: 2. Of those that a mesh axis runs over, the one named last changes fastest.
Arguments:
- merged: bfloat16 [768, 5120], P('dp'), may hold values from -6 to 6
- counts: int32 [8], P('dp'), may hold values from 4 to 384
- owners: int32 [768, 1], P('dp'), may hold values from 0 to 3; in each aligned block of 192 rows (0 to 191, 192 to 383, ...) at most 96 rows name the same one
- w_merge: bfloat16 [5120, 8192], P(None, ('group', 'section', 'tensor')), may hold values from -0.078125 to 0.078125
- norm_gain: float32 [8192], P(('group', 'section', 'tensor')), may hold values from 0.25 to 1.75
- cotangent: bfloat16 [4, 4, 96, 8192], P('dp', None, None, ('group', 'section', 'tensor')), may hold values from -6 to 6
Outputs:
- embedded: bfloat16 [4, 4, 96, 8192], P('dp', None, None, ('group', 'section', 'tensor'))
- grad_merged: float32 [768, 5120], P('dp', ('group', 'section', 'tensor'))
- grad_weight: float32 [5120, 8192], P('dp', ('group', 'section', 'tensor'))
Inputs may be any that keep to these rules, and one draw needn't show every extreme that they name: `owners`: in each replica's 192 rows no owner appears more than 96 times.
All inputs are finite; a program needn't handle non-finite values.
Results may differ from a plain program's by a relative error of at most 0.0049.
Values may be sent and summed in bfloat16 or wider, within the bound.
A program may use at most 64 MiB of HBM per device.

v0:
```python
import jax
import jax.numpy as jnp
from jax import lax
from jax.sharding import PartitionSpec as P

D = 8192


def on_device(merged, counts, owners, w_merge, norm_gain, cotangent):
    rows = merged.shape[0]
    columns = w_merge.shape[1]
    replicas = lax.axis_size("dp")
    slots = cotangent.shape[2]
    images = counts.shape[0]
    per_image = rows // images
    projected = jnp.dot(merged, w_merge, preferred_element_type=jnp.float32).astype(jnp.bfloat16)
    row_index = jnp.arange(rows, dtype=jnp.int32)
    image_of = row_index // per_image
    picked = image_of[:, None] == jnp.arange(images, dtype=jnp.int32)[None, :]
    count_of = jnp.sum(jnp.where(picked, counts[None, :], 0), axis=1)
    valid = (4 * (row_index % per_image) < count_of).astype(jnp.float32)
    masked = (projected.astype(jnp.float32) * valid[:, None]).astype(jnp.bfloat16)
    owner = owners[:, 0]
    hits = (owner[:, None] == jnp.arange(replicas, dtype=jnp.int32)[None, :]).astype(jnp.int32)
    before = jnp.cumsum(hits, axis=0) - hits
    slot_index = jnp.sum(before * hits, axis=1)
    target = owner * slots + slot_index
    placer = (jnp.arange(replicas * slots, dtype=jnp.int32)[:, None] == target[None, :]).astype(
        jnp.bfloat16
    )
    outgoing = jnp.dot(placer, masked, preferred_element_type=jnp.float32).astype(jnp.bfloat16)
    outgoing = outgoing.reshape(replicas, slots, columns)
    received = lax.all_to_all(outgoing, "dp", split_axis=0, concat_axis=0, tiled=True)
    values = received.astype(jnp.float32)
    square_sums = lax.psum(jnp.sum(values * values, axis=2), ("group", "section", "tensor"))
    scale = lax.rsqrt(square_sums / D + 1e-05)
    normed = (values * scale[:, :, None] * norm_gain[None, None, :]).astype(jnp.bfloat16)
    embedded = normed[None]
    grad_in = cotangent[0].astype(jnp.float32) * norm_gain[None, None, :]
    inner_sums = lax.psum(jnp.sum(grad_in * values, axis=2), ("group", "section", "tensor"))
    inner = inner_sums / D
    slot_grad = (scale[:, :, None] * grad_in - values * (scale**3 * inner)[:, :, None]).astype(
        jnp.bfloat16
    )
    returned = lax.all_to_all(slot_grad, "dp", split_axis=0, concat_axis=0, tiled=True)
    returned = returned.reshape(replicas * slots, columns)
    gathered = lax.dot_general(
        placer, returned, (((0,), (0,)), ((), ())), preferred_element_type=jnp.float32
    )
    back = (gathered * valid[:, None]).astype(jnp.bfloat16)
    input_terms = lax.dot_general(
        back, w_merge, (((1,), (1,)), ((), ())), preferred_element_type=jnp.float32
    )
    grad_merged = lax.psum_scatter(
        input_terms, ("group", "section", "tensor"), scatter_dimension=1, tiled=True
    )
    column_block = lax.all_to_all(merged, "dp", split_axis=1, concat_axis=0, tiled=True)
    grad_weight = lax.dot_general(
        column_block,
        lax.all_gather(back, "dp", axis=0, tiled=True),
        (((0,), (0,)), ((), ())),
        preferred_element_type=jnp.float32,
    )
    return (embedded, grad_merged, grad_weight)


def solution(mesh):
    placed = (
        P("dp", None),
        P("dp"),
        P("dp", None),
        P(None, ("group", "section", "tensor")),
        P(("group", "section", "tensor")),
        P("dp", None, None, ("group", "section", "tensor")),
    )
    return jax.shard_map(
        on_device,
        mesh=mesh,
        in_specs=placed,
        out_specs=(
            P("dp", None, None, ("group", "section", "tensor")),
            P("dp", ("group", "section", "tensor")),
            P("dp", ("group", "section", "tensor")),
        ),
        check_vma=False,
    )
```

profile of v0, /device:TPU:0, one launch (start us, length us, event | category | flops | bytes accessed | tf_op | source)
XLA Modules:
  0.0 182.4 jit_solution(6930971145670902794)
XLA Ops:
  8.0 0.0 all-gather.2.cloned.1.call-start
  8.1 0.7 iota_compare_fusion.3
  8.7 0.7 fusion.18
  9.5 1.2 reduce-window.6
  10.8 0.1 slice.12
  10.8 0.1 copy.23
  11.0 0.1 copy.24
  11.1 0.1 add_bitcast_fusion
  11.2 0.7 fusion.16
  11.9 0.7 multiply_add_fusion
  12.5 0.0 copy-start.2
  12.5 7.0 %convolution_convert_fusion = bf16[384,1024]{1,0:T(8,128)(2,1)S(1)} fusion(bf16[192,5120]{1,0:T(8,128)(2,1)} %param.6, bf16[5120,1024]{1,0:T(8,128)(2,1)} %param.9, f32[192]{0:T(256)S(1)} %compare_convert_fusion, s32[192]{0:T(256)S(1)} %multiply_add_fusion), kind=kOutput, calls=%fused_computation.14 | convolution fusion | flops 2165514240 | bytes 13239808 | tf_op jit(solution)/shard_map/dot_general | solution.py:31
  19.6 0.0 copy-start
  19.6 26.4 %all_to_all.29 = bf16[4,96,1024]{2,1,0:T(8,128)(2,1)S(1)} all-to-all(bf16[4,96,1024]{2,1,0:T(8,128)(2,1)S(1)} %bitcast.38), channel_id=1, replica_groups=mesh['group'=2,'dp'=4,'section'=2,'tensor'=2] {'dp'}, dimensions={0} | all-to-all | bytes 1572864 | tf_op jit(solution)/shard_map/all_to_all | solution.py:33
  46.0 0.0 copy-done.2
  46.0 0.0 copy-done
  46.0 0.4 fusion.3
  46.4 14.3 %all-reduce.1 = (f32[4,96]{1,0:T(4,128)S(1)}, f32[4,96]{1,0:T(4,128)S(1)}) all-reduce(f32[4,96]{1,0:T(4,128)S(1)} %get-tuple-element.19, f32[4,96]{1,0:T(4,128)S(1)} %get-tuple-element.18), channel_id=1, replica_groups=mesh['group'=2,'dp'=4,'section'=2,'tensor'=2] {'group','section','tensor'}, use_global_device_ids=true, to_apply=%region_5.6 | all-reduce | flops 768 | bytes 6144 | tf_op jit(solution)/shard_map/psum | solution.py:35
  60.7 1.4 fusion.5
  62.1 23.6 %all_to_all.30 = bf16[4,96,1024]{2,1,0:T(8,128)(2,1)S(1)} all-to-all(bf16[4,96,1024]{2,1,0:T(8,128)(2,1)S(1)} %get-tuple-element.22), channel_id=1, replica_groups=mesh['group'=2,'dp'=4,'section'=2,'tensor'=2] {'dp'}, dimensions={0} | all-to-all | bytes 1572864 | tf_op jit(solution)/shard_map/all_to_all | solution.py:45
  85.7 1.2 fusion.7
  86.9 0.0 all-gather.2.cloned.1.call-update
  86.9 0.0 reduce-scatter.2.cloned.1.call-start
  86.9 9.7 %fusion.21 = f32[192,5120]{1,0:T(8,128)} fusion(bf16[192,1024]{1,0:T(8,128)(2,1)} %fusion.7, bf16[5120,1024]{1,0:T(8,128)(2,1)} %param.9), kind=kOutput, calls=%fused_computation.48 | convolution fusion | flops 2013265920 | bytes 14811136 | tf_op jit(solution)/shard_map/dot_general | solution.py:51
  96.7 0.0 copy-start.1
  96.7 0.0 reduce-scatter.2.cloned.1.call-update
  96.7 1.5 copy-done.1
  98.2 0.1 copy.31
  98.3 64.7 %all_to_all.31 = bf16[192,4,1280]{2,0,1:T(8,128)(2,1)S(1)} all-to-all(bf16[192,4,1280]{2,0,1:T(8,128)(2,1)S(1)} %bitcast.34), channel_id=1, replica_groups=mesh['group'=2,'dp'=4,'section'=2,'tensor'=2] {'dp'}, dimensions={1} | all-to-all | bytes 3932160 | tf_op jit(solution)/shard_map/all_to_all | solution.py:57
  163.1 0.0 all-gather.2.cloned.1.call-done
  163.1 6.0 %convolution_bitcast_fusion = f32[1280,1024]{0,1:T(8,128)} fusion(bf16[768,1024]{1,0:T(8,128)(2,1)} %all-gather.2.cloned.1.call-done, bf16[768,1280]{1,0:T(8,128)(2,1)S(1)} %bitcast.37), kind=kOutput, calls=%fused_computation | convolution fusion | flops 2013265920 | bytes 8781824 | tf_op jit(solution)/shard_map/dot_general | solution.py:58
  169.1 5.9 %copy.26 = f32[1280,1024]{1,0:T(8,128)} copy(f32[1280,1024]{0,1:T(8,128)} %convolution_bitcast_fusion) | data formatting | bytes 10485760
  174.9 0.0 reduce-scatter.2.cloned.1.call-done
  (8 shorter events, 0.1 us)
Async XLA Ops:
  8.0 155.1 %all-gather.2.cloned.1.call-start = ((), (), s32[]{:S(2)}) async-start(), calls=%async_computation.5 | async-start | bytes 1966080 | tf_op jit(solution)/shard_map/all_gather | solution.py:60
  12.5 33.4 %copy-start.2 = (f32[1024]{0:T(1024)S(1)}, f32[1024]{0:T(1024)}, u32[]{:S(2)}) copy-start(f32[1024]{0:T(1024)} %param.10) | copy-start | bytes 12292
  19.6 26.4 %copy-start = (bf16[1,4,96,1024]{3,2,1,0:T(8,128)(2,1)S(1)}, bf16[1,4,96,1024]{3,2,1,0:T(8,128)(2,1)}, u32[]{:S(2)}) copy-start(bf16[1,4,96,1024]{3,2,1,0:T(8,128)(2,1)} %param.11) | copy-start | bytes 2359300
  86.9 88.1 %reduce-scatter.2.cloned.1.call-start = ((), (), s32[]{:S(2)}) async-start(), calls=%async_computation.4 | async-start | bytes 4423680 | tf_op jit(solution)/shard_map/reduce_scatter | solution.py:54
  96.7 1.5 copy-start.1
Sparse Core Ops, SparseCore 0:
  87.0 58.4 all-gather.1
Sparse Core Ops, SparseCore 1:
  96.8 46.7 reduce-scatter.1
where the time goes:
time: 183 us; the launch traced here: 182 us
  blocking collectives  129 us (70%)
  matrix products  23.9 us (13%)
  between operations  15.5 us (8%)
  local copies, waits for them, and re-layouts  7.84 us (4%)
  other arithmetic  6.04 us (3%)
    all_to_all x1, blocking collectives, on_device(): lax.all_to_all(merged, 'dp', split_axis=1, concat_axis=0, tiled=True)  64.7 us
    all_to_all x1, blocking collectives, on_device(): lax.all_to_all(outgoing, 'dp', split_axis=0, concat_axis=0, tiled=True)  26.4 us
    all_to_all x1, blocking collectives, on_device(): lax.all_to_all(slot_grad, 'dp', split_axis=0, concat_axis=0, tiled=True)  23.6 us
    psum x1, blocking collectives, on_device(): lax.psum(jnp.sum(values * values, axis=2), ('group', 'section', 'tensor'))  14.3 us
    dot_general x1, matrix products, on_device(): lax.dot_general(back, w_merge, (((1,), (1,)), ((), ())), preferred_elemen...  9.72 us
    unnamed x8, local copies, waits for them, and re-layouts  7.42 us
    dot_general x1, matrix products, on_device(): jnp.dot(placer, masked, preferred_element_type=jnp.float32)  7.02 us
    dot_general x1, matrix products, on_device(): lax.dot_general(column_block, lax.all_gather(back, 'dp', axis=0, tiled=Tr...  5.97 us
  transfers between devices with their start and end apart: 2, of which 0 were waited for; matrix products, arithmetic and copies ran while one was open for 12% of the time, Pallas kernels for 0%

commit v1 on v0

--- a/solution.py
+++ b/solution.py
@@ -32,7 +32,9 @@
     outgoing = outgoing.reshape(replicas, slots, columns)
     received = lax.all_to_all(outgoing, "dp", split_axis=0, concat_axis=0, tiled=True)
     values = received.astype(jnp.float32)
-    square_sums = lax.psum(jnp.sum(values * values, axis=2), ("group", "section", "tensor"))
+    square_sums = lax.psum(
+        lax.psum(jnp.sum(values * values, axis=2), "group"), ("section", "tensor")
+    )
     scale = lax.rsqrt(square_sums / D + 1e-05)
     normed = (values * scale[:, :, None] * norm_gain[None, None, :]).astype(jnp.bfloat16)
     embedded = normed[None]

time: 183 us -> 193 us (1.055)
  blocking collectives: 129 us -> 140 us
    psum x1 -> x3, blocking collectives: 14.3 us -> 26.3 us  [the longest x1 14.3 us: on_device(): lax.psum(jnp.sum(grad_in * values, axis=2), ('group', 'section', 'tensor'))]
    all_to_all x1, blocking collectives: 23.6 us -> 21.1 us  [on_device(): lax.all_to_all(slot_grad, 'dp', split_axis=0, concat_axis=0, tiled=True)]
  transfers between devices with their start and end apart: 2 -> 2, of which waited for: 0 -> 0; matrix products, arithmetic and copies ran while one was open for 12% -> 11% of each run, Pallas kernels for 0% -> 0%
where the time goes in v1:
time: 193 us
  blocking collectives  140 us (73%)
  matrix products  23.8 us (12%)
  between operations  15.5 us (8%)
  local copies, waits for them, and re-layouts  7.84 us (4%)
  other arithmetic  6.04 us (3%)
    all_to_all x1, blocking collectives, on_device(): lax.all_to_all(merged, 'dp', split_axis=1, concat_axis=0, tiled=True)  65.8 us
    all_to_all x1, blocking collectives, on_device(): lax.all_to_all(outgoing, 'dp', split_axis=0, concat_axis=0, tiled=True)  26.4 us
    all_to_all x1, blocking collectives, on_device(): lax.all_to_all(slot_grad, 'dp', split_axis=0, concat_axis=0, tiled=True)  21.1 us
    psum x1, blocking collectives, on_device(): lax.psum(jnp.sum(grad_in * values, axis=2), ('group', 'section', 'tensor'))  14.3 us
    dot_general x1, matrix products, on_device(): lax.dot_general(back, w_merge, (((1,), (1,)), ((), ())), preferred_elemen...  9.66 us
    psum x1, blocking collectives, on_device(): lax.psum(lax.psum(jnp.sum(values * values, axis=2), 'group'), ('section',...  9.29 us
    unnamed x8, local copies, waits for them, and re-layouts  7.42 us
    dot_general x1, matrix products, on_device(): jnp.dot(placer, masked, preferred_element_type=jnp.float32)  7.02 us
  transfers between devices with their start and end apart: 2, of which 0 were waited for; matrix products, arithmetic and copies ran while one was open for 11% of the time, Pallas kernels for 0%

profile of v1, /device:TPU:0, one launch (start us, length us, event | category | flops | bytes accessed | tf_op | source)
XLA Modules:
  0.0 192.9 jit_solution(674671091930638997)
XLA Ops:
  8.0 0.0 all-gather.2.cloned.1.call-start
  8.1 0.7 iota_compare_fusion.3
  8.7 0.7 fusion.18
  9.5 1.2 reduce-window.6
  10.8 0.1 slice.12
  10.8 0.1 copy.23
  11.0 0.1 copy.24
  11.1 0.1 add_bitcast_fusion
  11.2 0.7 fusion.16
  11.9 0.7 multiply_add_fusion
  12.5 0.0 copy-start.2
  12.5 7.0 %convolution_convert_fusion = bf16[384,1024]{1,0:T(8,128)(2,1)S(1)} fusion(bf16[192,5120]{1,0:T(8,128)(2,1)} %param.6, bf16[5120,1024]{1,0:T(8,128)(2,1)} %param.9, f32[192]{0:T(256)S(1)} %compare_convert_fusion, s32[192]{0:T(256)S(1)} %multiply_add_fusion), kind=kOutput, calls=%fused_computation.14 | convolution fusion | flops 2165514240 | bytes 13239808 | tf_op jit(solution)/shard_map/dot_general | solution.py:31
  19.6 0.0 copy-start
  19.6 26.4 %all_to_all.29 = bf16[4,96,1024]{2,1,0:T(8,128)(2,1)S(1)} all-to-all(bf16[4,96,1024]{2,1,0:T(8,128)(2,1)S(1)} %bitcast.38), channel_id=1, replica_groups=mesh['group'=2,'dp'=4,'section'=2,'tensor'=2] {'dp'}, dimensions={0} | all-to-all | bytes 1572864 | tf_op jit(solution)/shard_map/all_to_all | solution.py:33
  46.0 0.0 copy-done.2
  46.0 0.0 copy-done
  46.0 0.4 fusion.3
  46.4 14.3 %psum.23 = f32[4,96]{1,0:T(4,128)S(1)} all-reduce(f32[4,96]{1,0:T(4,128)S(1)} %get-tuple-element.18), channel_id=1, replica_groups=mesh['group'=2,'dp'=4,'section'=2,'tensor'=2] {'group','section','tensor'}, use_global_device_ids=true, to_apply=%region_8.9 | all-reduce | flops 384 | bytes 3072 | tf_op jit(solution)/shard_map/psum | solution.py:42
  60.7 2.8 %psum.21 = f32[4,96]{1,0:T(4,128)S(1)} all-reduce(f32[4,96]{1,0:T(4,128)S(1)} %get-tuple-element.19), channel_id=1, replica_groups=mesh['group'=2,'dp'=4,'section'=2,'tensor'=2] {'group'}, use_global_device_ids=true, to_apply=%region_5.6 | all-reduce | flops 384 | bytes 3072 | tf_op jit(solution)/shard_map/psum | solution.py:36
  63.5 9.3 %psum.22 = f32[4,96]{1,0:T(4,128)S(1)} all-reduce(f32[4,96]{1,0:T(4,128)S(1)} %psum.21), channel_id=1, replica_groups=mesh['group'=2,'dp'=4,'section'=2,'tensor'=2] {'section','tensor'}, use_global_device_ids=true, to_apply=%region_6.7 | all-reduce | flops 384 | bytes 3072 | tf_op jit(solution)/shard_map/psum | solution.py:35
  72.8 1.4 fusion.5
  74.2 21.1 %all_to_all.30 = bf16[4,96,1024]{2,1,0:T(8,128)(2,1)S(1)} all-to-all(bf16[4,96,1024]{2,1,0:T(8,128)(2,1)S(1)} %get-tuple-element.20), channel_id=1, replica_groups=mesh['group'=2,'dp'=4,'section'=2,'tensor'=2] {'dp'}, dimensions={0} | all-to-all | bytes 1572864 | tf_op jit(solution)/shard_map/all_to_all | solution.py:47
  95.3 1.2 fusion.7
  96.4 0.0 all-gather.2.cloned.1.call-update
  96.5 0.0 reduce-scatter.2.cloned.1.call-start
  96.5 9.7 %fusion.21 = f32[192,5120]{1,0:T(8,128)} fusion(bf16[192,1024]{1,0:T(8,128)(2,1)} %fusion.7, bf16[5120,1024]{1,0:T(8,128)(2,1)} %param.9), kind=kOutput, calls=%fused_computation.48 | convolution fusion | flops 2013265920 | bytes 14811136 | tf_op jit(solution)/shard_map/dot_general | solution.py:53
  106.2 0.0 copy-start.1
  106.2 0.0 reduce-scatter.2.cloned.1.call-update
  106.2 1.5 copy-done.1
  107.7 0.1 copy.31
  107.8 65.8 %all_to_all.31 = bf16[192,4,1280]{2,0,1:T(8,128)(2,1)S(1)} all-to-all(bf16[192,4,1280]{2,0,1:T(8,128)(2,1)S(1)} %bitcast.34), channel_id=1, replica_groups=mesh['group'=2,'dp'=4,'section'=2,'tensor'=2] {'dp'}, dimensions={1} | all-to-all | bytes 3932160 | tf_op jit(solution)/shard_map/all_to_all | solution.py:59
  173.6 0.0 all-gather.2.cloned.1.call-done
  173.6 6.0 %convolution_bitcast_fusion = f32[1280,1024]{0,1:T(8,128)} fusion(bf16[768,1024]{1,0:T(8,128)(2,1)} %all-gather.2.cloned.1.call-done, bf16[768,1280]{1,0:T(8,128)(2,1)S(1)} %bitcast.37), kind=kOutput, calls=%fused_computation | convolution fusion | flops 2013265920 | bytes 8781824 | tf_op jit(solution)/shard_map/dot_general | solution.py:60
  179.6 5.9 %copy.26 = f32[1280,1024]{1,0:T(8,128)} copy(f32[1280,1024]{0,1:T(8,128)} %convolution_bitcast_fusion) | data formatting | bytes 10485760
  185.5 0.0 reduce-scatter.2.cloned.1.call-done
  (8 shorter events, 0.1 us)
Async XLA Ops:
  8.0 165.6 %all-gather.2.cloned.1.call-start = ((), (), s32[]{:S(2)}) async-start(), calls=%async_computation.5 | async-start | bytes 1966080 | tf_op jit(solution)/shard_map/all_gather | solution.py:62
  12.5 33.4 %copy-start.2 = (f32[1024]{0:T(1024)S(1)}, f32[1024]{0:T(1024)}, u32[]{:S(2)}) copy-start(f32[1024]{0:T(1024)} %param.10) | copy-start | bytes 12292
  19.6 26.4 %copy-start = (bf16[1,4,96,1024]{3,2,1,0:T(8,128)(2,1)S(1)}, bf16[1,4,96,1024]{3,2,1,0:T(8,128)(2,1)}, u32[]{:S(2)}) copy-start(bf16[1,4,96,1024]{3,2,1,0:T(8,128)(2,1)} %param.11) | copy-start | bytes 2359300
  96.5 89.0 %reduce-scatter.2.cloned.1.call-start = ((), (), s32[]{:S(2)}) async-start(), calls=%async_computation.4 | async-start | bytes 4423680 | tf_op jit(solution)/shard_map/reduce_scatter | solution.py:56
  106.2 1.5 copy-start.1
Sparse Core Ops, SparseCore 0:
  96.6 61.3 all-gather.1
Sparse Core Ops, SparseCore 1:
  106.3 47.7 reduce-scatter.1
